TPU v7x, 512 devices: a whole 4x8x8 slice. The times are simulated.
512 devices in a mesh: section: 2 (over core), tensor: 32 (over z, x), dp: 8 (over y).
Axes of the slice: x: 4, y: 8, z: 8, core: 2. Of those that a mesh axis runs over, the one named last changes fastest.
Arguments:
- grad_out: bfloat16 [2048, 6144], P('dp', 'tensor'), may hold values from -6 to 6
- queries: bfloat16 [2, 2048, 4096], P('section', 'dp', 'tensor'), may hold values from -40 to 40
- key_rows: bfloat16 [2, 2048, 4096], P('section', 'dp', 'tensor'), may hold values from -40 to 40
- value_rows: bfloat16 [2, 2048, 4096], P('section', 'dp', 'tensor'), may hold values from -6 to 6
- w_qkv: bfloat16 [2, 6144, 12288], P('section', 'dp', 'tensor'), may hold values from -0.078125 to 0.078125
- w_out: bfloat16 [2, 4096, 6144], P('section', 'tensor', 'dp'), may hold values from -0.09375 to 0.09375
- seg_lengths: int32 [8, 3], P('dp'), may hold values from 0 to 128, as said below
Outputs:
- input_grad: bfloat16 [2, 2048, 6144], P('section', 'dp', 'tensor')
- out_weight_grad: bfloat16 [2, 4096, 6144], P('section', 'tensor', 'dp')
Inputs may be any that keep to these rules, and one draw needn't show every extreme that they name: `seg_lengths`: each row sums to 256, holds one image of exactly 128 patches and either a second of 128 patches and an empty last slot, or two of 64 patches.
All inputs are finite; a program needn't handle non-finite values.
Results may differ from a plain program's by a relative error of at most 0.023.
Values may be sent and summed in bfloat16 or wider, within the bound.
A program may use at most 64 MiB of HBM per device.

v0:
```python
import jax
import jax.numpy as jnp
from jax import lax
from jax.sharding import PartitionSpec as P

PACK = 256
MB = 1
negative_big = -1e30


def passed_along(value, axis, steps):
    count = lax.axis_size(axis)
    first, last = (max(0, -steps), min(count, count - steps))
    return lax.ppermute(value, axis, [(source, source + steps) for source in range(first, last)])


def contract(left, right, left_dim, right_dim):
    return lax.dot_general(
        left, right, (((left_dim,), (right_dim,)), ((), ())), preferred_element_type=jnp.float32
    )


def attend_back(query_blk, key_blk, value_blk, grad_attn, same_seg, scaling):
    scores = contract(query_blk, key_blk, 1, 1) * scaling
    scores = jnp.where(same_seg, scores, negative_big)
    peak = jnp.max(scores, axis=-1, keepdims=True)
    shifted = jnp.exp(scores - peak)
    probs = shifted / jnp.sum(shifted, axis=-1, keepdims=True)
    probs_low = probs.astype(jnp.bfloat16)
    attended = jnp.dot(probs_low, value_blk, preferred_element_type=jnp.float32).astype(
        jnp.bfloat16
    )
    grad_value = contract(probs_low, grad_attn, 0, 0).astype(jnp.bfloat16)
    grad_probs = contract(grad_attn, value_blk, 1, 1)
    centred = jnp.sum(probs * grad_probs, axis=-1, keepdims=True)
    grad_scores = (probs * (grad_probs - centred) * scaling).astype(jnp.bfloat16)
    grad_query = jnp.dot(grad_scores, key_blk, preferred_element_type=jnp.float32).astype(
        jnp.bfloat16
    )
    grad_key = contract(grad_scores, query_blk, 0, 0).astype(jnp.bfloat16)
    return (attended, grad_query, grad_key, grad_value)


def per_device(grad_out, queries, key_rows, value_rows, w_qkv, w_out, seg_lengths):
    sections = lax.axis_size("section")
    section_index = lax.axis_index("section")
    head_index = lax.axis_index("tensor")
    width = grad_out.shape[1]
    qkv_full, out_full = (
        lax.all_gather(w_qkv, "dp", axis=1, tiled=True),
        lax.all_gather(w_out, "dp", axis=2, tiled=True),
    )
    proj_in = qkv_full[0]
    proj_out = out_full[0]
    head_dim = proj_out.shape[0]
    full_width = proj_out.shape[1]
    scaling = head_dim ** (-0.5)
    seg_ends = jnp.cumsum(seg_lengths, axis=1)
    position = jnp.arange(PACK, dtype=jnp.int32)
    seg_table = jnp.sum((position[None, :, None] >= seg_ends[:, None, :]).astype(jnp.int32), axis=2)
    offset = sections - 1 - section_index
    carried = jnp.zeros((PACK, width), jnp.bfloat16)
    result = jnp.zeros((MB * PACK, width), jnp.bfloat16)
    grad_acc = jnp.zeros((head_dim, full_width), jnp.float32)
    for step_index in range(MB + sections - 1):
        micro = step_index - offset
        active = (micro >= 0) & (micro < MB)
        which = jnp.clip(micro, 0, MB - 1)
        incoming = jnp.where(section_index == sections - 1, grad_out, carried)
        whole = lax.all_gather(incoming, "tensor", axis=1, tiled=True)
        query_blk = queries[0]
        key_blk = key_rows[0]
        value_blk = value_rows[0]
        seg_ids = lax.dynamic_index_in_dim(seg_table, which, 0, keepdims=False)
        same_seg = seg_ids[:, None] == seg_ids[None, :]
        grad_attn = contract(whole, proj_out, 1, 1).astype(jnp.bfloat16)
        attended, grad_query, grad_key, grad_value = attend_back(
            query_blk, key_blk, value_blk, grad_attn, same_seg, scaling
        )
        combined = jnp.concatenate([grad_query, grad_key, grad_value], axis=1)
        head_term = contract(combined, proj_in, 1, 1)
        summed = lax.psum(head_term.astype(jnp.bfloat16), "tensor").astype(jnp.float32)
        share = lax.dynamic_slice_in_dim(summed, head_index * width, width, 1)
        block_grad = (incoming.astype(jnp.float32) + share).astype(jnp.bfloat16)
        result = jnp.where(active, block_grad, result)
        grad_acc = grad_acc + jnp.where(active, contract(attended, whole, 0, 0), 0.0)
        carried = passed_along(block_grad, "section", -1)
    weight_share = lax.psum_scatter(
        grad_acc.astype(jnp.bfloat16), "dp", scatter_dimension=1, tiled=True
    )
    return (result[None], weight_share[None])


def solution(mesh):
    return jax.shard_map(
        per_device,
        mesh=mesh,
        in_specs=(
            P("dp", "tensor"),
            P("section", "dp", "tensor"),
            P("section", "dp", "tensor"),
            P("section", "dp", "tensor"),
            P("section", "dp", "tensor"),
            P("section", "tensor", "dp"),
            P("dp", None),
        ),
        out_specs=(P("section", "dp", "tensor"), P("section", "tensor", "dp")),
        check_vma=False,
    )
```

profile of v0, /device:TPU:6, one launch (start us, length us, event | category | flops | bytes accessed | tf_op | source)
XLA Modules:
  0.0 695.8 jit_solution(12003352529557310799)
XLA Ops:
  7.2 0.0 copy-start
  7.2 0.0 all-gather.7.cloned.1.call-start
  7.2 0.7 all-gather.7.cloned.1.call-update
  7.9 0.0 all-gather.5.cloned.1.call-start
  8.0 0.7 broadcast_select_fusion.1
  8.6 0.0 all-gather.5.cloned.1.call-update
  8.7 0.0 all-gather.9.cloned.1.call-start
  8.7 0.7 all-gather.9.cloned.1.call-update
  9.4 0.0 all-reduce.3.cloned.1.call-start
  9.4 0.8 reduce_window_sum.11
  10.3 0.1 fusion.40
  10.4 1.1 fusion.49
  11.5 0.1 fusion.16
  11.5 0.0 copy-start.8
  11.5 0.0 copy-start.9
  11.5 45.2 %all-gather.7.cloned.1.call-done = bf16[1,128,6144]{2,1,0:T(8,128)(2,1)} async-done(((bf16[1,128,768]{2,1,0:T(8,128)(2,1)}), bf16[1,128,6144]{2,1,0:T(8,128)(2,1)}) %all-gather.7.cloned.1.call-update) | async-done | bytes 1572880 | tf_op jit(solution)/shard_map/all_gather | solution.py:51
  56.7 86.7 %all-gather.5.cloned.1.call-done = bf16[256,6144]{0,1:T(8,128)(2,1)} async-done(((bf16[256,192]{0,1:T(8,128)(2,1)}), bf16[256,6144]{0,1:T(8,128)(2,1)}) %all-gather.5.cloned.1.call-update) | async-done | bytes 3145744 | tf_op jit(solution)/shard_map/all_gather | solution.py:70
  143.4 3.4 fusion.9
  146.8 0.0 copy-done
  146.8 0.2 multiply_reduce_fusion.1
  147.1 0.1 multiply_convert_fusion.1
  147.1 0.0 copy-done.8
  147.1 0.2 convolution_convert_fusion.7
  147.3 0.0 copy-done.9
  147.3 0.2 convolution_convert_fusion.8
  147.6 0.2 convolution_convert_fusion.6
  147.7 57.7 %all-gather.9.cloned.1.call-done = bf16[1,6144,384]{2,1,0:T(8,128)(2,1)} async-done(((bf16[1,768,384]{2,1,0:T(8,128)(2,1)}), bf16[1,6144,384]{2,1,0:T(8,128)(2,1)}) %all-gather.9.cloned.1.call-update) | async-done | bytes 4718608 | tf_op jit(solution)/shard_map/all_gather | solution.py:50
  205.5 5.9 convolution_convert_fusion.1
  211.4 0.0 copy-start.4
  211.4 0.0 copy-start.3
  211.4 0.0 all-reduce.3.cloned.1.call-update
  211.4 0.0 all-gather.11.cloned.1.call-start
  211.5 168.1 %all-reduce.3.cloned.1.call-done = bf16[256,6144]{0,1:T(8,128)(2,1)} async-done(((bf16[256,6144]{0,1:T(8,128)(2,1)}), bf16[256,6144]{0,1:T(8,128)(2,1)}) %all-reduce.3.cloned.1.call-update) | async-done | bytes 3145744 | tf_op jit(solution)/shard_map/psum | solution.py:82
  379.6 0.0 copy-done.4
  379.6 0.9 add_convert_fusion.1
  380.5 0.0 copy-start.6
  380.5 1.3 collective-permute-start
  381.8 1.9 collective-permute-done
  383.7 0.7 broadcast_select_fusion
  384.4 0.0 all-gather.11.cloned.1.call-update
  384.4 0.0 all-reduce.5.cloned.1.call-start
  384.4 82.7 %all-gather.11.cloned.1.call-done = bf16[256,6144]{0,1:T(8,128)(2,1)} async-done(((bf16[256,192]{0,1:T(8,128)(2,1)}), bf16[256,6144]{0,1:T(8,128)(2,1)}) %all-gather.11.cloned.1.call-update) | async-done | bytes 3145744 | tf_op jit(solution)/shard_map/all_gather | solution.py:70
  467.2 0.0 copy-done.3
  467.2 2.9 fusion.12
  470.1 0.2 convolution_convert_fusion.3
  470.3 0.2 multiply_reduce_fusion
  470.5 0.0 copy-done.6
  470.5 0.1 multiply_convert_fusion
  470.6 0.2 convolution_convert_fusion.4
  470.8 0.2 convolution_convert_fusion.5
  471.0 5.9 convolution_convert_fusion
  477.0 0.0 all-reduce.5.cloned.1.call-update
  477.0 0.0 reduce-scatter.2.cloned.1.call-start
  477.0 0.2 convolution_convert_fusion.2
  477.3 1.6 copy-done.1
  478.8 1.2 convolution_select_fusion.1
  480.0 0.7 copy-done.2
  480.7 2.3 fusion.1
  483.1 0.0 reduce-scatter.2.cloned.1.call-update
  483.1 160.8 %all-reduce.5.cloned.1.call-done = bf16[256,6144]{0,1:T(8,128)(2,1)} async-done(((bf16[256,6144]{0,1:T(8,128)(2,1)}), bf16[256,6144]{0,1:T(8,128)(2,1)}) %all-reduce.5.cloned.1.call-update) | async-done | bytes 3145744 | tf_op jit(solution)/shard_map/psum | solution.py:82
  644.0 0.0 copy-done.5
  644.0 0.0 copy-done.7
  644.0 1.6 fusion.28
  645.5 43.4 %reduce-scatter.2.cloned.1.call-done = bf16[128,768]{1,0:T(8,128)(2,1)} async-done(((bf16[128,6144]{1,0:T(8,128)(2,1)}), bf16[128,768]{1,0:T(8,128)(2,1)}) %reduce-scatter.2.cloned.1.call-update) | async-done | bytes 196624 | tf_op jit(solution)/shard_map/reduce_scatter | solution.py:88
  (4 shorter events, 0.0 us)
Async XLA Ops:
  7.2 139.7 %copy-start = (bf16[1,256,128]{2,1,0:T(8,128)(2,1)S(1)}, bf16[1,256,128]{2,1,0:T(8,128)(2,1)}, u32[]{:S(2)}) copy-start(bf16[1,256,128]{2,1,0:T(8,128)(2,1)} %param.10) | copy-start | bytes 196612
  7.2 49.5 %all-gather.7.cloned.1.call-start = ((), (), s32[]{:S(2)}) async-start(), calls=%async_computation.2 | async-start | bytes 1769472 | tf_op jit(solution)/shard_map/all_gather | solution.py:51
  7.9 135.5 %all-gather.5.cloned.1.call-start = ((), (), s32[]{:S(2)}) async-start(), calls=%async_computation.1 | async-start | bytes 3244032 | tf_op jit(solution)/shard_map/all_gather | solution.py:70
  8.7 196.8 %all-gather.9.cloned.1.call-start = ((), (), s32[]{:S(2)}) async-start(), calls=%async_computation.3 | async-start | bytes 5308416 | tf_op jit(solution)/shard_map/all_gather | solution.py:50
  9.4 370.2 %all-reduce.3.cloned.1.call-start = ((), (), s32[]{:S(2)}) async-start(), calls=%async_computation.4 | async-start | bytes 6291456 | tf_op jit(solution)/shard_map/psum | solution.py:82
  11.5 135.6 %copy-start.8 = (bf16[1,256,128]{2,1,0:T(8,128)(2,1)S(1)}, bf16[1,256,128]{2,1,0:T(8,128)(2,1)}, u32[]{:S(2)}) copy-start(bf16[1,256,128]{2,1,0:T(8,128)(2,1)} %param.8) | copy-start | bytes 196612
  11.5 135.8 %copy-start.9 = (bf16[1,256,128]{2,1,0:T(8,128)(2,1)S(1)}, bf16[1,256,128]{2,1,0:T(8,128)(2,1)}, u32[]{:S(2)}) copy-start(bf16[1,256,128]{2,1,0:T(8,128)(2,1)} %param.9) | copy-start | bytes 196612
  211.4 168.2 %copy-start.4 = (bf16[256,192]{0,1:T(8,128)(2,1)S(1)}, bf16[256,192]{0,1:T(8,128)(2,1)}, u32[]{:S(2)}) copy-start(bf16[256,192]{0,1:T(8,128)(2,1)} %param.7) | copy-start | bytes 294916
  211.4 255.8 %copy-start.3 = (bf16[1,128,6144]{2,1,0:T(8,128)(2,1)S(1)}, bf16[1,128,6144]{2,1,0:T(8,128)(2,1)}, u32[]{:S(2)}) copy-start(bf16[1,128,6144]{2,1,0:T(8,128)(2,1)} %all-gather.7.cloned.1.call-done) | copy-start | bytes 4718596
  211.4 255.8 %all-gather.11.cloned.1.call-start = ((), (), s32[]{:S(2)}) async-start(), calls=%async_computation.5 | async-start | bytes 3244032 | tf_op jit(solution)/shard_map/all_gather | solution.py:70
  380.5 90.0 %copy-start.6 = (bf16[256,192]{0,1:T(8,128)(2,1)}, bf16[256,192]{0,1:T(8,128)(2,1)S(1)}, u32[]{:S(2)}) copy-start(bf16[256,192]{0,1:T(8,128)(2,1)S(1)} %add_convert_fusion.1) | copy-start | bytes 294916
  380.5 3.2 collective-permute-start
  384.4 259.6 %all-reduce.5.cloned.1.call-start = ((), (), s32[]{:S(2)}) async-start(), calls=%async_computation.6 | async-start | bytes 6291456 | tf_op jit(solution)/shard_map/psum | solution.py:82
  477.0 1.9 copy-start.1
  477.0 212.0 %reduce-scatter.2.cloned.1.call-start = ((), (), s32[]{:S(2)}) async-start(), calls=%async_computation.7 | async-start | bytes 1769472 | tf_op jit(solution)/shard_map/reduce_scatter | solution.py:88
  478.8 1.9 copy-start.2
  480.7 163.2 %copy-start.5 = (bf16[256,192]{0,1:T(8,128)(2,1)S(1)}, bf16[256,192]{0,1:T(8,128)(2,1)}, u32[]{:S(2)}) copy-start(bf16[256,192]{0,1:T(8,128)(2,1)} %broadcast_select_fusion) | copy-start | bytes 294916
  480.7 163.2 %copy-start.7 = (bf16[256,192]{0,1:T(8,128)(2,1)S(1)}, bf16[256,192]{0,1:T(8,128)(2,1)}, u32[]{:S(2)}) copy-start(bf16[256,192]{0,1:T(8,128)(2,1)} %copy-done.6) | copy-start | bytes 294916
Sparse Core Ops, SparseCore 0:
  10.1 46.5 all-gather.6
  60.4 82.9 all-gather.4
  145.5 59.8 all-gather.8
  211.5 167.9 all-reduce.2
  384.5 82.6 all-gather.10
  477.1 166.8 all-reduce.4
  647.4 41.5 reduce-scatter.1
where the time goes:
time: 696 us
  waiting for transfers between devices  648 us (93%)
  matrix products  24.6 us (4%)
  between operations  14.3 us (2%)
    psum x2, waiting for transfers between devices, per_device(): lax.psum(head_term.astype(jnp.bfloat16), 'tensor').astype(jnp.float32)  329 us
    all_gather x2, waiting for transfers between devices, per_device(): whole = lax.all_gather(incoming, 'tensor', axis=1, tiled=True)  169 us
    all_gather x1, waiting for transfers between devices, per_device(): lax.all_gather(w_qkv, 'dp', axis=1, tiled=True)  57.7 us
    all_gather x1, waiting for transfers between devices, per_device(): lax.all_gather(w_out, 'dp', axis=2, tiled=True)  45.2 us
    reduce_scatter x1, waiting for transfers between devices, per_device(): lax.psum_scatter(grad_acc.astype(jnp.bfloat16), 'dp', scatter_dimension=1...  43.4 us
    dot_general x13, matrix products, contract(): lax.dot_general(left, right, (((left_dim,), (right_dim,)), ((), ())), pre...  23.9 us
  transfers between devices with their start and end apart: 8, of which 8 were waited for; matrix products, arithmetic and copies ran while one was open for 2% of the time, Pallas kernels for 0%

commit v1 on v0

--- a/solution.py
+++ b/solution.py
@@ -6,6 +6,24 @@
 PACK = 256
 MB = 1
 negative_big = -1e30
+
+
+def gather_around(value, axis, dim):
+    ways, here, lap = (lax.axis_size(axis), lax.axis_index(axis), value.shape[dim])
+    shape = [n * ways if d == dim else n for d, n in enumerate(value.shape)]
+    full = lax.dynamic_update_slice_in_dim(
+        jnp.zeros(shape, value.dtype), value, here * lap, axis=dim
+    )
+    going_up = going_down = value
+    for far in range(1, ways // 2 + 1):
+        going_up = lax.ppermute(going_up, axis, [(d, (d + 1) % ways) for d in range(ways)])
+        full = lax.dynamic_update_slice_in_dim(full, going_up, (here - far) % ways * lap, axis=dim)
+        if 2 * far < ways:
+            going_down = lax.ppermute(going_down, axis, [(d, (d - 1) % ways) for d in range(ways)])
+            full = lax.dynamic_update_slice_in_dim(
+                full, going_down, (here + far) % ways * lap, axis=dim
+            )
+    return full
 
 
 def passed_along(value, axis, steps):
@@ -48,7 +66,7 @@
     width = grad_out.shape[1]
     qkv_full, out_full = (
         lax.all_gather(w_qkv, "dp", axis=1, tiled=True),
-        lax.all_gather(w_out, "dp", axis=2, tiled=True),
+        gather_around(w_out, "dp", 2),
     )
     proj_in = qkv_full[0]
     proj_out = out_full[0]

time: 696 us -> 653 us (0.938)
  waiting for transfers between devices: 648 us -> 581 us
  starting transfers between devices: 1.57 us -> 24.8 us
    all_gather x1 -> x0, waiting for transfers between devices: 45.2 us -> none  [per_device(): lax.all_gather(w_out, 'dp', axis=2, tiled=True)]
    all_gather x2, waiting for transfers between devices: 169 us -> 135 us  [per_device(): whole = lax.all_gather(incoming, 'tensor', axis=1, tiled=True)]
    ppermute x0 -> x7, starting transfers between devices: none -> 23.3 us  [the longest x3 14.1 us: gather_around(): lax.ppermute(going_down, axis, [(d, (d - 1) % ways) for d in range(ways)])]
    ppermute x0 -> x7, waiting for transfers between devices: none -> 13.2 us  [the longest x4 13.2 us: gather_around(): lax.ppermute(going_up, axis, [(d, (d + 1) % ways) for d in range(ways)])]
  transfers between devices with their start and end apart: 8 -> 14, of which waited for: 8 -> 11; matrix products, arithmetic and copies ran while one was open for 2% -> 2% of each run, Pallas kernels for 0% -> 0%
where the time goes in v1:
time: 653 us; the launch traced here: 652 us
  waiting for transfers between devices  581 us (89%)
  starting transfers between devices  24.8 us (4%)
  matrix products  24 us (4%)
  between operations  14.6 us (2%)
    psum x2, waiting for transfers between devices, per_device(): lax.psum(head_term.astype(jnp.bfloat16), 'tensor').astype(jnp.float32)  329 us
    all_gather x2, waiting for transfers between devices, per_device(): whole = lax.all_gather(incoming, 'tensor', axis=1, tiled=True)  135 us
    all_gather x1, waiting for transfers between devices, per_device(): lax.all_gather(w_qkv, 'dp', axis=1, tiled=True)  58.2 us
    reduce_scatter x1, waiting for transfers between devices, per_device(): lax.psum_scatter(grad_acc.astype(jnp.bfloat16), 'dp', scatter_dimension=1...  43.3 us
    dot_general x13, matrix products, contract(): lax.dot_general(left, right, (((left_dim,), (right_dim,)), ((), ())), pre...  23.3 us
    ppermute x3, starting transfers between devices, gather_around(): lax.ppermute(going_down, axis, [(d, (d - 1) % ways) for d in range(ways)])  14.1 us
    ppermute x4, waiting for transfers between devices, gather_around(): lax.ppermute(going_up, axis, [(d, (d + 1) % ways) for d in range(ways)])  13.2 us
  transfers between devices with their start and end apart: 14, of which 11 were waited for; matrix products, arithmetic and copies ran while one was open for 2% of the time, Pallas kernels for 0%

profile of v1, /device:TPU:6, one launch (start us, length us, event | category | flops | bytes accessed | tf_op | source)
XLA Modules:
  0.0 652.5 jit_solution(17170259759607919953)
XLA Ops:
  7.2 0.0 copy-start
  7.2 0.0 copy-start.9
  7.2 0.0 all-gather.4.cloned.1.call-start
  7.2 0.7 broadcast_select_fusion.1
  7.9 0.0 all-gather.4.cloned.1.call-update
  7.9 0.0 all-gather.6.cloned.1.call-start
  8.0 0.7 all-gather.6.cloned.1.call-update
  8.7 0.0 all-reduce.3.cloned.1.call-start
  8.7 3.5 collective-permute-start
  12.2 3.8 collective-permute-start.1
  16.2 0.8 reduce_window_sum.11
  17.0 0.1 fusion.30
  17.1 1.1 fusion.39
  18.2 0.1 fusion.6
  18.3 0.1 squeeze.39
  18.4 1.5 collective-permute-done
  20.0 1.9 collective-permute-start.2
  21.9 5.1 collective-permute-start.3
  27.1 2.9 collective-permute-done.2
  30.0 1.9 collective-permute-start.4
  31.9 0.0 collective-permute-done.3
  31.9 5.1 collective-permute-start.5
  37.1 2.0 collective-permute-done.4
  39.1 1.9 collective-permute-start.6
  41.1 6.8 %collective-permute-done.6 = bf16[1,128,768]{2,1,0:T(8,128)(2,1)S(1)} collective-permute-done((bf16[1,128,768]{2,1,0:T(8,128)(2,1)S(1)}, bf16[1,128,768]{2,1,0:T(8,128)(2,1)S(1)}, u32[]{:S(2)}, u32[]{:S(2)}) %collective-permute-start.6) | collective-permute-done | bytes 196640 | tf_op jit(solution)/shard_map/ppermute | solution.py:19
  47.9 0.0 copy-start.7
  47.9 0.0 copy-start.8
  48.0 52.4 %all-gather.4.cloned.1.call-done = bf16[256,6144]{0,1:T(8,128)(2,1)} async-done(((bf16[256,192]{0,1:T(8,128)(2,1)}), bf16[256,6144]{0,1:T(8,128)(2,1)}) %all-gather.4.cloned.1.call-update) | async-done | bytes 3145744 | tf_op jit(solution)/shard_map/all_gather | solution.py:88
  100.4 2.9 convolution_convert_fusion.3
  103.3 0.2 multiply_reduce_fusion.1
  103.5 0.1 multiply_convert_fusion.1
  103.6 0.2 convolution_convert_fusion.9
  103.8 0.2 convolution_convert_fusion.10
  104.0 0.2 convolution_convert_fusion.8
  104.2 58.2 %all-gather.6.cloned.1.call-done = bf16[1,6144,384]{2,1,0:T(8,128)(2,1)} async-done(((bf16[1,768,384]{2,1,0:T(8,128)(2,1)}), bf16[1,6144,384]{2,1,0:T(8,128)(2,1)}) %all-gather.6.cloned.1.call-update) | async-done | bytes 4718608 | tf_op jit(solution)/shard_map/all_gather | solution.py:68
  162.4 5.9 convolution_convert_fusion.1
  168.3 0.0 all-reduce.3.cloned.1.call-update
  168.4 0.0 all-gather.8.cloned.1.call-start
  168.4 168.1 %all-reduce.3.cloned.1.call-done = bf16[256,6144]{0,1:T(8,128)(2,1)} async-done(((bf16[256,6144]{0,1:T(8,128)(2,1)}), bf16[256,6144]{0,1:T(8,128)(2,1)}) %all-reduce.3.cloned.1.call-update) | async-done | bytes 3145744 | tf_op jit(solution)/shard_map/psum | solution.py:100
  336.5 0.9 add_convert_fusion.1
  337.4 1.3 collective-permute-start.7
  338.7 1.9 collective-permute-done.7
  340.6 0.7 broadcast_select_fusion
  341.3 0.0 all-gather.8.cloned.1.call-update
  341.3 0.0 all-reduce.5.cloned.1.call-start
  341.3 82.7 %all-gather.8.cloned.1.call-done = bf16[256,6144]{0,1:T(8,128)(2,1)} async-done(((bf16[256,192]{0,1:T(8,128)(2,1)}), bf16[256,6144]{0,1:T(8,128)(2,1)}) %all-gather.8.cloned.1.call-update) | async-done | bytes 3145744 | tf_op jit(solution)/shard_map/all_gather | solution.py:88
  424.1 2.9 convolution_convert_fusion.2
  427.0 0.2 convolution_convert_fusion.5
  427.2 0.2 multiply_reduce_fusion
  427.4 0.1 multiply_convert_fusion
  427.5 0.2 convolution_convert_fusion.6
  427.7 0.2 convolution_convert_fusion.7
  427.9 5.9 convolution_convert_fusion
  433.8 0.0 all-reduce.5.cloned.1.call-update
  433.8 0.0 reduce-scatter.2.cloned.1.call-start
  433.9 0.2 convolution_convert_fusion.4
  434.2 1.6 copy-done.1
  435.7 1.2 convolution_select_fusion.1
  436.9 0.7 copy-done.2
  437.6 2.3 fusion.1
  439.9 0.0 reduce-scatter.2.cloned.1.call-update
  439.9 160.9 %all-reduce.5.cloned.1.call-done = bf16[256,6144]{0,1:T(8,128)(2,1)} async-done(((bf16[256,6144]{0,1:T(8,128)(2,1)}), bf16[256,6144]{0,1:T(8,128)(2,1)}) %all-reduce.5.cloned.1.call-update) | async-done | bytes 3145744 | tf_op jit(solution)/shard_map/psum | solution.py:100
  600.8 1.6 fusion.18
  602.4 43.3 %reduce-scatter.2.cloned.1.call-done = bf16[128,768]{1,0:T(8,128)(2,1)} async-done(((bf16[128,6144]{1,0:T(8,128)(2,1)}), bf16[128,768]{1,0:T(8,128)(2,1)}) %reduce-scatter.2.cloned.1.call-update) | async-done | bytes 196624 | tf_op jit(solution)/shard_map/reduce_scatter | solution.py:106
  (24 shorter events, 0.2 us)
Async XLA Ops:
  7.2 96.1 %copy-start = (bf16[1,256,128]{2,1,0:T(8,128)(2,1)S(1)}, bf16[1,256,128]{2,1,0:T(8,128)(2,1)}, u32[]{:S(2)}) copy-start(bf16[1,256,128]{2,1,0:T(8,128)(2,1)} %param.10) | copy-start | bytes 196612
  7.2 11.2 %copy-start.9 = (bf16[1,128,768]{2,1,0:T(8,128)(2,1)S(1)}, bf16[1,128,768]{2,1,0:T(8,128)(2,1)}, u32[]{:S(2)}) copy-start(bf16[1,128,768]{2,1,0:T(8,128)(2,1)} %param.12) | copy-start | bytes 589828
  7.2 93.2 %all-gather.4.cloned.1.call-start = ((), (), s32[]{:S(2)}) async-start(), calls=%async_computation.1 | async-start | bytes 3244032 | tf_op jit(solution)/shard_map/all_gather | solution.py:88
  7.9 154.5 %all-gather.6.cloned.1.call-start = ((), (), s32[]{:S(2)}) async-start(), calls=%async_computation.2 | async-start | bytes 5308416 | tf_op jit(solution)/shard_map/all_gather | solution.py:68
  8.7 327.8 %all-reduce.3.cloned.1.call-start = ((), (), s32[]{:S(2)}) async-start(), calls=%async_computation.3 | async-start | bytes 6291456 | tf_op jit(solution)/shard_map/psum | solution.py:100
  8.7 11.2 %collective-permute-start = (bf16[1,128,768]{2,1,0:T(8,128)(2,1)}, bf16[1,128,768]{2,1,0:T(8,128)(2,1)S(1)}, u32[]{:S(2)}, u32[]{:S(2)}) collective-permute-start(bf16[1,128,768]{2,1,0:T(8,128)(2,1)} %param.12), channel_id=1, source_target_pairs={{0,1},{1,2},{2,3},{3,4},{4,5},{5,6},{6,7},{7,0},{8,9},{9,10},{10,1... | collective-permute-start | bytes 589832 | tf_op jit(solution)/shard_map/ppermute | solution.py:19
  12.2 9.7 %collective-permute-start.1 = (bf16[1,128,768]{2,1,0:T(8,128)(2,1)}, bf16[1,128,768]{2,1,0:T(8,128)(2,1)S(1)}, u32[]{:S(2)}, u32[]{:S(2)}) collective-permute-start(bf16[1,128,768]{2,1,0:T(8,128)(2,1)} %param.12), channel_id=1, source_target_pairs={{0,7},{1,0},{2,1},{3,2},{4,3},{5,4},{6,5},{7,6},{8,15},{9,8},{10,9... | collective-permute-start | bytes 589832 | tf_op jit(solution)/shard_map/ppermute | solution.py:22
  20.0 10.0 %collective-permute-start.2 = (bf16[1,128,768]{2,1,0:T(8,128)(2,1)S(1)}, bf16[1,128,768]{2,1,0:T(8,128)(2,1)S(1)}, u32[]{:S(2)}, u32[]{:S(2)}) collective-permute-start(bf16[1,128,768]{2,1,0:T(8,128)(2,1)S(1)} %collective-permute-done), channel_id=1, source_target_pairs={{0,1},{1,2},{2,3},{3,4},{4,5},{5,6},{6,7},{7,0},{8,9},{9,10},{10,1... | collective-permute-start | bytes 589832 | tf_op jit(solution)/shard_map/ppermute | solution.py:19
  21.9 10.0 %collective-permute-start.3 = (bf16[1,128,768]{2,1,0:T(8,128)(2,1)S(1)}, bf16[1,128,768]{2,1,0:T(8,128)(2,1)S(1)}, u32[]{:S(2)}, u32[]{:S(2)}) collective-permute-start(bf16[1,128,768]{2,1,0:T(8,128)(2,1)S(1)} %collective-permute-done.1), channel_id=1, source_target_pairs={{0,7},{1,0},{2,1},{3,2},{4,3},{5,4},{6,5},{7,6},{8,15},{9,8},{10,9... | collective-permute-start | bytes 589832 | tf_op jit(solution)/shard_map/ppermute | solution.py:22
  30.0 9.2 %collective-permute-start.4 = (bf16[1,128,768]{2,1,0:T(8,128)(2,1)S(1)}, bf16[1,128,768]{2,1,0:T(8,128)(2,1)S(1)}, u32[]{:S(2)}, u32[]{:S(2)}) collective-permute-start(bf16[1,128,768]{2,1,0:T(8,128)(2,1)S(1)} %collective-permute-done.2), channel_id=1, source_target_pairs={{0,1},{1,2},{2,3},{3,4},{4,5},{5,6},{6,7},{7,0},{8,9},{9,10},{10,1... | collective-permute-start | bytes 589832 | tf_op jit(solution)/shard_map/ppermute | solution.py:19
  31.9 9.2 %collective-permute-start.5 = (bf16[1,128,768]{2,1,0:T(8,128)(2,1)S(1)}, bf16[1,128,768]{2,1,0:T(8,128)(2,1)S(1)}, u32[]{:S(2)}, u32[]{:S(2)}) collective-permute-start(bf16[1,128,768]{2,1,0:T(8,128)(2,1)S(1)} %collective-permute-done.3), channel_id=1, source_target_pairs={{0,7},{1,0},{2,1},{3,2},{4,3},{5,4},{6,5},{7,6},{8,15},{9,8},{10,9... | collective-permute-start | bytes 589832 | tf_op jit(solution)/shard_map/ppermute | solution.py:22
  39.1 8.8 %collective-permute-start.6 = (bf16[1,128,768]{2,1,0:T(8,128)(2,1)S(1)}, bf16[1,128,768]{2,1,0:T(8,128)(2,1)S(1)}, u32[]{:S(2)}, u32[]{:S(2)}) collective-permute-start(bf16[1,128,768]{2,1,0:T(8,128)(2,1)S(1)} %collective-permute-done.4), channel_id=1, source_target_pairs={{0,1},{1,2},{2,3},{3,4},{4,5},{5,6},{6,7},{7,0},{8,9},{9,10},{10,1... | collective-permute-start | bytes 589832 | tf_op jit(solution)/shard_map/ppermute | solution.py:19
  47.9 55.7 %copy-start.7 = (bf16[1,256,128]{2,1,0:T(8,128)(2,1)S(1)}, bf16[1,256,128]{2,1,0:T(8,128)(2,1)}, u32[]{:S(2)}) copy-start(bf16[1,256,128]{2,1,0:T(8,128)(2,1)} %param.8) | copy-start | bytes 196612
  47.9 55.9 %copy-start.8 = (bf16[1,256,128]{2,1,0:T(8,128)(2,1)S(1)}, bf16[1,256,128]{2,1,0:T(8,128)(2,1)}, u32[]{:S(2)}) copy-start(bf16[1,256,128]{2,1,0:T(8,128)(2,1)} %param.9) | copy-start | bytes 196612
  168.3 168.1 %copy-start.3 = (bf16[256,192]{0,1:T(8,128)(2,1)S(1)}, bf16[256,192]{0,1:T(8,128)(2,1)}, u32[]{:S(2)}) copy-start(bf16[256,192]{0,1:T(8,128)(2,1)} %param.7) | copy-start | bytes 294916
  168.4 255.7 %all-gather.8.cloned.1.call-start = ((), (), s32[]{:S(2)}) async-start(), calls=%async_computation.4 | async-start | bytes 3244032 | tf_op jit(solution)/shard_map/all_gather | solution.py:88
  337.4 90.0 %copy-start.5 = (bf16[256,192]{0,1:T(8,128)(2,1)}, bf16[256,192]{0,1:T(8,128)(2,1)S(1)}, u32[]{:S(2)}) copy-start(bf16[256,192]{0,1:T(8,128)(2,1)S(1)} %add_convert_fusion.1) | copy-start | bytes 294916
  337.4 3.2 collective-permute-start.7
  341.3 259.5 %all-reduce.5.cloned.1.call-start = ((), (), s32[]{:S(2)}) async-start(), calls=%async_computation.5 | async-start | bytes 6291456 | tf_op jit(solution)/shard_map/psum | solution.py:100
  433.8 1.9 copy-start.1
  433.8 211.8 %reduce-scatter.2.cloned.1.call-start = ((), (), s32[]{:S(2)}) async-start(), calls=%async_computation.6 | async-start | bytes 1769472 | tf_op jit(solution)/shard_map/reduce_scatter | solution.py:106
  435.7 1.9 copy-start.2
  437.6 163.2 %copy-start.4 = (bf16[256,192]{0,1:T(8,128)(2,1)S(1)}, bf16[256,192]{0,1:T(8,128)(2,1)}, u32[]{:S(2)}) copy-start(bf16[256,192]{0,1:T(8,128)(2,1)} %broadcast_select_fusion) | copy-start | bytes 294916
  437.6 163.2 %copy-start.6 = (bf16[256,192]{0,1:T(8,128)(2,1)S(1)}, bf16[256,192]{0,1:T(8,128)(2,1)}, u32[]{:S(2)}) copy-start(bf16[256,192]{0,1:T(8,128)(2,1)} %copy-done.5) | copy-start | bytes 294916
Sparse Core Ops, SparseCore 0:
  11.7 88.5 all-gather.3
  102.5 59.9 all-gather.5
  168.5 167.9 all-reduce.2
  341.4 82.6 all-gather.7
  434.0 166.8 all-reduce.4
  604.1 41.5 reduce-scatter.1
